TPU v7x, 256 devices: a whole 4x4x8 slice. The times are simulated.
256 devices in a mesh: pair: 128 (over y_lo, z, x, core), trow: 2 (over y_hi).
Axes of the slice: x: 4, y: 4 (y_hi: 2, y_lo: 2; y = y_hi * 2 + y_lo), z: 8, core: 2. Of those that a mesh axis runs over, the one named last changes fastest.
Arguments:
- query_bank: bfloat16 [128, 64, 1024], P('pair'), may hold values from -6 to 6
- ref_owner: int32 [1], replicated, may hold values from 0 to 127
- target_feat: bfloat16 [128, 512, 1024], P('pair', None, 'trow'), may hold values from -60 to 60
- valid_rows: int32 [128], P('pair'), may hold values from 2 to 16, as said below
- w_first: bfloat16 [16, 1, 3, 3, 3, 3], replicated, may hold values from -2 to 2
- b_first: float32 [16], replicated, may hold values from -0.5 to 0.5
- w_middle: bfloat16 [16, 16, 3, 3, 3, 3], replicated, may hold values from -0.25 to 0.25
- b_middle: float32 [16], replicated, may hold values from -0.5 to 0.5
- w_last: bfloat16 [1, 16, 3, 3, 3, 3], replicated, may hold values from -0.25 to 0.25
- b_last: float32 [1], replicated, may hold values from -0.5 to 0.5
Outputs:
- scores: float32 [128, 64, 512], P('pair', None, 'trow')
Inputs may be any that keep to these rules, and one draw needn't show every extreme that they name: ref_owner names the group along pair whose window is the reference. Rows of a target grid at or past valid_rows are padding; some pair fills all 16 rows.
All inputs are finite; a program needn't handle non-finite values.
Results may differ from a plain program's by a relative error of at most 0.007.
Values may be sent and summed in bfloat16 or wider, within the bound.
A program may use at most 64 MiB of HBM per device.

v0:
```python
import math

import jax
import jax.numpy as jnp
from jax import lax
from jax.sharding import PartitionSpec as P

WB = 32
WA = 32


EPS_NORM = 1e-06
EPS_PEAK = 1e-05


def extended(cells, sides, width):
    for axis, dim in sides:
        count = lax.axis_size(axis)
        ends = count - 1
        head = lax.slice_in_dim(cells, 0, width, axis=dim)
        tail = lax.slice_in_dim(cells, cells.shape[dim] - width, cells.shape[dim], axis=dim)
        cells = jnp.concatenate(
            [
                lax.ppermute(tail, axis, [(i, (i + 1) % count) for i in range(ends)]),
                cells,
                lax.ppermute(head, axis, [((i + 1) % count, i) for i in range(ends)]),
            ],
            axis=dim,
        )
    return cells


def broadcast(shard, axis, root):
    mine = lax.axis_index(axis) == root
    return lax.psum(jnp.where(mine, shard, jnp.zeros_like(shard)), axis)


def shift_along(values, offset, axis_dim):
    if offset == 0:
        return values
    length = values.shape[axis_dim]
    zero_shape = list(values.shape)
    zero_shape[axis_dim] = abs(offset)
    zero_block = jnp.zeros(zero_shape, values.dtype)
    if offset > 0:
        return jnp.concatenate(
            [lax.slice_in_dim(values, offset, length, axis=axis_dim), zero_block], axis=axis_dim
        )
    return jnp.concatenate(
        [zero_block, lax.slice_in_dim(values, 0, length + offset, axis=axis_dim)], axis=axis_dim
    )


def block_conv(row_block, weight_matrix, out_channels, block_rows):
    extent = row_block.shape[2]
    column_pos = jnp.arange(extent, dtype=jnp.int32) % WB
    shifted = []
    for col_off in (-1, 0, 1):
        in_range = (column_pos + col_off >= 0) & (column_pos + col_off < WB)
        moved_cols = shift_along(row_block, col_off, 2)
        shifted.append(
            jnp.where(in_range[None, None, :], moved_cols, jnp.zeros((), row_block.dtype))
        )
    layers = []
    for row_off in range(3):
        for col_idx in range(3):
            layers.append(
                lax.slice_in_dim(
                    shifted[col_idx], row_off * WB, (row_off + block_rows) * WB, axis=2
                )
            )
    stacked = jnp.concatenate(layers, axis=0)
    products = jnp.einsum("pk,kab->pab", weight_matrix, stacked, preferred_element_type=jnp.float32)
    positions = row_block.shape[1]
    query_row = jnp.arange(positions, dtype=jnp.int32) // WA
    query_col = jnp.arange(positions, dtype=jnp.int32) % WA
    ref_rows = positions // WA
    accumulated = jnp.zeros((out_channels, positions, block_rows * WB), jnp.float32)
    for row_off in range(3):
        for col_off in range(3):
            start_chan = (row_off * 3 + col_off) * out_channels
            offset_group = products[start_chan : start_chan + out_channels]
            in_range = (query_row + row_off - 1 >= 0) & (query_row + row_off - 1 < ref_rows)
            in_range = in_range & (query_col + col_off - 1 >= 0) & (query_col + col_off - 1 < WA)
            moved_group = shift_along(offset_group, (row_off - 1) * WA + col_off - 1, 1)
            accumulated = accumulated + jnp.where(in_range[None, :, None], moved_group, 0.0)
    return accumulated


def conv_layer(inputs, weight, bias):
    out_channels = weight.shape[0]
    in_channels = weight.shape[1]
    weight_matrix = jnp.transpose(weight, (2, 3, 0, 4, 5, 1)).reshape(
        9 * out_channels, 9 * in_channels
    )
    rows_out = inputs.shape[2] // WB - 2
    block_rows = 1
    for option in (2, 4):
        block_rows = option

    def one_block(block_index):
        row_block = lax.dynamic_slice_in_dim(
            inputs, block_index * (block_rows * WB), (block_rows + 2) * WB, 2
        )
        return block_conv(row_block, weight_matrix, out_channels, block_rows)

    block_outputs = lax.map(one_block, jnp.arange(rows_out // block_rows, dtype=jnp.int32))
    joined = jnp.transpose(block_outputs, (1, 2, 0, 3)).reshape(
        out_channels, inputs.shape[1], rows_out * WB
    )
    return joined + bias[:, None, None]


def unit_rows(features):
    values = features.astype(jnp.float32)
    return (values * lax.rsqrt(jnp.sum(values * values, axis=1, keepdims=True) + EPS_NORM)).astype(
        jnp.bfloat16
    )


def contract(left, right):
    return lax.dot_general(
        left, right, (((1,), (1,)), ((), ())), preferred_element_type=jnp.float32
    )


def score_pair(raw_dot, squares, trow_rank, row_count, cos_scale, weights):
    w_first, b_first, w_middle, b_middle, w_last, b_last = weights
    rows_here = raw_dot.shape[1] // WB
    first_row = trow_rank * rows_here
    global_row = first_row + jnp.arange(raw_dot.shape[1], dtype=jnp.int32) // WB
    is_live = global_row < row_count
    correlation = jnp.where(
        is_live[None, :], cos_scale * raw_dot * lax.rsqrt(squares + EPS_NORM)[None, :], 0.0
    )
    magnitude = jnp.abs(correlation)
    peak_query = jnp.max(magnitude, axis=0)
    peak_target = lax.pmax(jnp.max(magnitude, axis=1), "trow")
    volume = (
        correlation
        * (correlation / (peak_query[None, :] + EPS_PEAK))
        * (correlation / (peak_target[:, None] + EPS_PEAK))
    )
    volume = volume.astype(jnp.bfloat16)[None]
    padded = extended(volume, (("trow", 2),), WB)
    hidden = jnp.maximum(conv_layer(padded, w_first, b_first), 0.0).astype(jnp.bfloat16)
    padded = extended(hidden, (("trow", 2),), WB)
    hidden = jnp.maximum(conv_layer(padded, w_middle, b_middle), 0.0).astype(jnp.bfloat16)
    padded = extended(hidden, (("trow", 2),), WB)
    result = conv_layer(padded, w_last, b_last)[0]
    return jnp.where(is_live[None, :], result, 0.0)


def per_device(
    query_bank,
    ref_owner,
    target_feat,
    valid_rows,
    w_first,
    b_first,
    w_middle,
    b_middle,
    w_last,
    b_last,
):
    query_vec = broadcast(query_bank[0], "pair", ref_owner[0])
    unit_query = unit_rows(query_vec)
    cos_scale = math.sqrt(query_vec.shape[1])
    trow_rank = lax.axis_index("trow")
    weights = (w_first, b_first, w_middle, b_middle, w_last, b_last)
    exchanged = lax.all_to_all(target_feat, "trow", split_axis=1, concat_axis=2, tiled=True)
    local_rows = exchanged[0]
    raw_dot = contract(unit_query, local_rows)
    squares = jnp.sum(jnp.square(local_rows.astype(jnp.float32)), axis=1)
    scores = [score_pair(raw_dot, squares, trow_rank, valid_rows[0], cos_scale, weights)]
    return jnp.stack(scores)


def solution(mesh):
    in_specs = (
        P("pair", None, None),
        P(),
        P("pair", None, "trow"),
        P("pair"),
        P(),
        P(),
        P(),
        P(),
        P(),
        P(),
    )
    out_specs = P("pair", None, "trow")
    return jax.shard_map(
        per_device, mesh=mesh, in_specs=in_specs, out_specs=out_specs, check_vma=False
    )
```

profile of v0, /device:TPU:1, one launch (start us, length us, event | category | flops | bytes accessed | tf_op | source)
XLA Modules:
  0.0 1038.0 jit_solution(17501619991861130497)
XLA Ops:
  7.2 0.7 select_bitcast_fusion
  7.9 1.9 copy.50
  9.7 0.5 broadcast.3951
  10.3 3.8 reduce.1
  14.1 1.1 reshape.509
  15.2 5.0 all-to-all-start
  20.9 935.9 %all-reduce.32.cloned.1.call-done = bf16[64,1024]{1,0:T(8,128)(2,1)} async-done(((bf16[64,1024]{1,0:T(8,128)(2,1)}), bf16[64,1024]{1,0:T(8,128)(2,1)}) %all-reduce.32.cloned.1.call-update) | async-done | bytes 131088 | tf_op jit(solution)/shard_map/psum | solution.py:35
  956.8 1.0 fusion.30
  957.8 0.5 reshape.510
  958.5 0.2 copy.31
  958.9 0.3 abs_reduce_fusion.1
  959.3 5.3 pmax.7
  964.7 4.3 collective-permute-start
  969.1 1.3 collective-permute-start.1
  970.5 4.6 collective-permute-done.1
  975.2 10.4 while.45
  975.3 0.6 dynamic_slice.71
  976.9 0.3 fusion.92
  977.6 0.5 concatenate.223
  978.1 0.8 convolution_bitcast_fusion.6
  979.2 1.2 fusion.97
  980.4 0.6 dynamic_slice.71
  982.1 0.3 fusion.92
  982.8 0.5 concatenate.223
  983.3 0.8 convolution_bitcast_fusion.6
  984.3 1.2 fusion.97
  985.9 1.7 collective-permute-start.2
  987.6 1.5 collective-permute-start.3
  989.3 0.2 reshape.503
  989.5 1.4 collective-permute-done.2
  990.9 5.3 collective-permute-done.3
  996.2 0.5 pad_maximum_fusion
  996.8 11.8 %while.46 = (s32[]{:T(128)}, f32[2,16,64,128]{3,1,2,0:T(8,128)S(1)}, s32[2]{0:T(128)S(1)}, bf16[16,64,320]{2,0,1:T(8,128)(2,1)S(1)}, bf16[144,144]{1,0:T(8,128)(...) while((s32[]{:T(128)}, f32[2,16,64,128]{3,1,2,0:T(8,128)S(1)}, s32[2]{0:T(128)S(1)}, ...), condition=%wide.region_9.10_spmd, body=%wide.region_8.9_spmd.sunk | while | flops 342569024 | bytes 24628092 | solution.py:107
  996.8 0.6 dynamic_slice.73
  998.1 0.5 constant_dynamic-slice_fusion.9
  998.5 0.2 pad_select_fusion.8
  998.9 0.2 dynamic-slice_select_fusion.4
  1000.4 0.8 convolution_bitcast_fusion.7
  1001.5 1.2 fusion.104
  1002.7 0.6 dynamic_slice.73
  1004.0 0.4 constant_dynamic-slice_fusion.9
  1004.4 0.2 pad_select_fusion.8
  1004.8 0.2 dynamic-slice_select_fusion.4
  1006.3 0.8 convolution_bitcast_fusion.7
  1007.4 1.2 fusion.104
  1009.0 1.5 collective-permute-start.4
  1010.5 1.3 collective-permute-start.5
  1012.5 1.2 collective-permute-done.4
  1013.7 5.3 collective-permute-done.5
  1019.1 0.5 pad_maximum_fusion.1
  1019.6 10.9 %while.47 = (s32[]{:T(128)}, f32[2,1,64,128]{3,2,1,0:T(8,128)S(1)}, s32[2]{0:T(128)S(1)}, bf16[16,64,320]{2,0,1:T(8,128)(2,1)S(1)}, bf16[9,144]{1,0:T(8,128)(2,1...) while((s32[]{:T(128)}, f32[2,1,64,128]{3,2,1,0:T(8,128)S(1)}, s32[2]{0:T(128)S(1)}, ...), condition=%wide.region_11.12_spmd, body=%wide.region_10.11_spmd.sunk | while | flops 21975112 | bytes 11917275 | solution.py:107
  1019.6 0.6 dynamic_slice.75
  1020.7 0.4 constant_dynamic-slice_fusion.10
  1021.2 0.2 pad_select_fusion.10
  1021.5 0.2 dynamic-slice_select_fusion.5
  1023.1 0.4 convolution_bitcast_fusion.8
  1023.7 1.3 fusion.111
  1025.1 0.6 dynamic_slice.75
  1026.2 0.4 constant_dynamic-slice_fusion.10
  1026.7 0.2 pad_select_fusion.10
  1027.0 0.2 dynamic-slice_select_fusion.5
  1028.5 0.4 convolution_bitcast_fusion.8
  1029.2 1.3 fusion.111
  1030.5 0.6 bitcast_select_fusion
  (166 shorter events, 10.0 us)
Async XLA Ops:
  6.5 950.2 %all-reduce.32.cloned.1.call-start = ((), (), s32[]{:S(2)}) async-start(), calls=%async_computation.1 | async-start | bytes 262144 | tf_op jit(solution)/shard_map/psum | solution.py:35
  15.2 942.6 %all-to-all-start = ((bf16[2,2,65536]{2,1,0:T(2,128)(2,1)}), bf16[2,2,65536]{2,1,0:T(2,128)(2,1)S(1)}, u32[]{:S(2)}, u32[]{:S(2)}) async-start(bf16[2,2,65536]{2,1,0:T(2,128)(2,1)} %reshape.509), calls=%async_computation | async-start | bytes 1048576 | tf_op jit(solution)/shard_map/all_to_all | solution.py:171
  957.8 1.1 copy-start
  958.4 12.0 %copy-start.2 = (bf16[16,1,3,3,3,3]{0,5,4,3,2,1:T(4,128)(2,1)S(1)}, bf16[16,1,3,3,3,3]{0,5,4,3,2,1:T(4,128)(2,1)}, u32[]{:S(2)}) copy-start(bf16[16,1,3,3,3,3]{0,5,4,3,2,1:T(4,128)(2,1)} %param.20) | copy-start | bytes 7780
  964.7 5.8 collective-permute-start
  969.1 6.0 collective-permute-start.1
  975.2 10.4 %copy-start.4 = (f32[16]{0:T(128)S(1)}, f32[16]{0:T(128)}, u32[]{:S(2)}) copy-start(f32[16]{0:T(128)} %param.21) | copy-start | bytes 196
  985.6 3.5 copy-start.1
  985.9 5.0 collective-permute-start.2
  987.6 8.6 collective-permute-start.3
  996.8 11.8 %copy-start.5 = (f32[16]{0:T(128)S(1)}, f32[16]{0:T(128)}, u32[]{:S(2)}) copy-start(f32[16]{0:T(128)} %param.23) | copy-start | bytes 196
  1008.6 3.1 copy-start.3
  1009.0 4.8 collective-permute-start.4
  1010.5 8.6 collective-permute-start.5
Sparse Core Ops, SparseCore 0:
  9.9 946.7 all-reduce.31
where the time goes:
time: 1040 us
  waiting for transfers between devices  954 us (92%)
  local copies, waits for them, and re-layouts  19 us (2%)
  other arithmetic  18.8 us (2%)
  starting transfers between devices  16.5 us (2%)
  between operations  15.7 us (2%)
    psum x1, waiting for transfers between devices, broadcast(): return lax.psum(jnp.where(mine, shard, jnp.zeros_like(shard)), axis)  936 us
  transfers between devices with their start and end apart: 8, of which 6 were waited for; matrix products, arithmetic and copies ran while one was open for 1% of the time, Pallas kernels for 0%

commit v1 on v0

v1 whole, which is shorter than its diff:
```python
import functools
import math

import jax
import jax.numpy as jnp
from jax import lax
from jax.experimental import pallas as pl
from jax.experimental.pallas import tpu as pltpu
from jax.sharding import PartitionSpec as P

MESH = pl.DeviceIdType.MESH
WB = 32
WA = 32
HB = 16
NB = HB * WB
NA = 64
EPS_NORM = 1e-06
EPS_PEAK = 1e-05
F32 = jnp.float32
BF16 = jnp.bfloat16

BLOCKS = 6
STEP = 6
SLOTS = 32


def nt(left, right):
    return lax.dot_general(left, right, (((1,), (1,)), ((), ())), preferred_element_type=F32)


def nn(left, right):
    return lax.dot_general(left, right, (((1,), (0,)), ((), ())), preferred_element_type=F32)


def iota(shape, dim):
    return lax.broadcasted_iota(jnp.int32, shape, dim)


def comm_kernel(n, places, owner_ref, q_ref, tf_ref, u_ref, other_ref, unit, recv, pick, gath, sems, feat_sems):
    per = SLOTS // places
    stride = n // places
    me = lax.axis_index("pair")
    plane = lax.axis_index("trow")
    is_place = lax.rem(me, stride) == 0
    my_place = me // stride

    barrier = pltpu.get_barrier_semaphore()

    def greet(pair, trow):
        @pl.when(jnp.logical_or(pair != me, trow != plane))
        def _():
            pl.semaphore_signal(barrier, inc=1, device_id=(pair, trow), device_id_type=MESH)

    @pl.loop(0, places)
    def _(p):
        greet(p * stride, plane)
        greet(p * stride, 1 - plane)

    greet(me, 1 - plane)

    @pl.when(is_place)
    def _():
        @pl.loop(0, n)
        def _(d):
            greet(d, plane)

    values = q_ref[0].astype(F32)
    scale = lax.rsqrt(jnp.sum(values * values, axis=1, keepdims=True) + EPS_NORM)
    normed = values * scale
    for half in range(2):
        for s in range(SLOTS):
            g, t = s // 4, s % 4
            piece = normed[8 * g : 8 * g + 8, 512 * half + 128 * t : 512 * half + 128 * t + 128]
            unit[half, s // per, 8 * (s % per) : 8 * (s % per) + 8, :] = piece.astype(BF16)

    @pl.when(is_place)
    def _():
        pl.semaphore_wait(barrier, (2 * n - 1) + (places - 1) + 1)

    @pl.when(jnp.logical_not(is_place))
    def _():
        pl.semaphore_wait(barrier, places + 1)

    features = pltpu.make_async_remote_copy(
        src_ref=tf_ref.at[0],
        dst_ref=other_ref,
        send_sem=feat_sems.at[0],
        recv_sem=feat_sems.at[1],
        device_id=(me, 1 - plane),
        device_id_type=MESH,
    )
    features.start()

    @pl.loop(0, places)
    def _(p):
        @pl.when(p * stride != me)
        def _():
            pltpu.make_async_remote_copy(
                src_ref=unit.at[plane, p],
                dst_ref=recv.at[me],
                send_sem=sems.at[0],
                recv_sem=sems.at[1],
                device_id=(p * stride, plane),
                device_id_type=MESH,
            ).start()

    @pl.when(is_place)
    def _():
        own = pltpu.make_async_copy(unit.at[plane, my_place], recv.at[me], sems.at[4])
        own.start()
        own.wait()
        rest = recv.at[pl.ds(0, n - 1)]
        pltpu.make_async_copy(rest, rest, sems.at[1]).wait()
        chosen = recv[owner_ref[0]]
        pick[...] = chosen
        gath[plane * places + my_place] = chosen

        @pl.loop(1, n)
        def _(o):
            pltpu.make_async_remote_copy(
                src_ref=pick,
                dst_ref=gath.at[plane * places + my_place],
                send_sem=sems.at[2],
                recv_sem=sems.at[3],
                device_id=(lax.rem(me + o, n), plane),
                device_id_type=MESH,
            ).start()

        @pl.loop(0, n)
        def _(o):
            pltpu.make_async_remote_copy(
                src_ref=pick,
                dst_ref=gath.at[plane * places + my_place],
                send_sem=sems.at[5],
                recv_sem=sems.at[3],
                device_id=(lax.rem(me + o, n), 1 - plane),
                device_id_type=MESH,
            ).start()

        part = gath.at[pl.ds(0, 2 * places - 1)]
        pltpu.make_async_copy(part, part, sems.at[3]).wait()
        part = recv.at[pl.ds(0, n - 1)]
        pltpu.make_async_copy(part, part, sems.at[2]).wait()
        pltpu.make_async_copy(recv, recv, sems.at[5]).wait()
        if places > 1:
            part = unit.at[0, pl.ds(0, places - 1)]
            pltpu.make_async_copy(part, part, sems.at[0]).wait()

    @pl.when(jnp.logical_not(is_place))
    def _():
        pltpu.make_async_copy(gath, gath, sems.at[3]).wait()
        part = unit.at[0]
        pltpu.make_async_copy(part, part, sems.at[0]).wait()

    for half in range(2):
        rows = []
        for g in range(8):
            tiles = []
            for t in range(4):
                s = 4 * g + t
                tiles.append(gath[half * places + s // per, 8 * (s % per) : 8 * (s % per) + 8, :].astype(F32))
            rows.append(jnp.concatenate(tiles, axis=1))
        u_ref[half] = jnp.concatenate(rows, axis=0).astype(BF16)

    features.wait()


def exchange(owner, bank, feats, n):
    places = min(SLOTS, n)
    per = SLOTS // places
    return pl.pallas_call(
        functools.partial(comm_kernel, n, places),
        out_shape=(
            jax.ShapeDtypeStruct((2, NA, 512), BF16),
            jax.ShapeDtypeStruct((NB, 512), BF16),
        ),
        in_specs=[
            pl.BlockSpec(memory_space=pltpu.SMEM),
            pl.BlockSpec(memory_space=pltpu.VMEM),
            pl.BlockSpec(memory_space=pl.ANY),
        ],
        out_specs=(
            pl.BlockSpec(memory_space=pltpu.VMEM),
            pl.BlockSpec(memory_space=pl.ANY),
        ),
        scratch_shapes=[
            pltpu.VMEM((2, places, per * 8, 128), BF16),
            pltpu.VMEM((n, per * 8, 128), BF16),
            pltpu.VMEM((per * 8, 128), BF16),
            pltpu.VMEM((2 * places, per * 8, 128), BF16),
            pltpu.SemaphoreType.DMA((6,)),
            pltpu.SemaphoreType.DMA((2,)),
        ],
        compiler_params=pltpu.CompilerParams(collective_id=0, has_side_effects=True),
        name="window_exchange",
    )(owner, bank, feats)


def spread_rows(src_ref, tmp):
    tmp[...] = jnp.zeros_like(tmp)
    for t in range(27):
        tmp[t, 0:3, 0:16] = src_ref[t].astype(F32)
    flat = tmp[...].reshape(216, 128).astype(BF16)
    take = (iota((128, 128), 1) % 16 == iota((128, 128), 0)).astype(F32).astype(BF16)
    return nn(flat, take)


def bias_row(b_ref, used):
    lane = iota((1, 256), 1)
    row = jnp.zeros((1, 256), F32)
    for o in range(16):
        row = jnp.where(lane % 16 == o, b_ref[o], row)
    return jnp.where(lane < used, row, 0.0)


def prepare(wf_ref, wm_ref, wl_ref, tmp, spread, w1, w2, w3):
    spread[0:216, :] = spread_rows(wf_ref, tmp)
    row = iota((32, 128), 0)
    lane = iota((32, 128), 1)
    for tile in range(2):
        j_of = row // 2 - (tile * 4 + lane // 32)
        i_of = row % 2 - (lane // 16) % 2 + 1
        for k in range(3):
            for l in range(4):
                block = jnp.zeros((32, 128), F32)
                if l < 3:
                    for i in range(3):
                        for j in range(3):
                            t = (i * 3 + j) * 3 + k
                            value = spread[8 * t + l : 8 * t + l + 1, :]
                            block = jnp.where((j_of == j) & (i_of == i), value, block)
                w1[k, 32 * l : 32 * l + 32, 128 * tile : 128 * tile + 128] = block.astype(BF16)

    spread[0:216, :] = spread_rows(wl_ref, tmp)
    w3[...] = jnp.zeros_like(w3)
    odd1 = (iota((1, 128), 1) // 16) % 2 == 1
    for half in range(2):
        for tile in range(12):
            m, first = tile // 2, (tile % 2) * 4
            columns = [6 * m + q for q in range(first, first + 4) if q < STEP and 6 * m + q < WA]
            if not columns or columns[-1] < 16 * half - 1 or columns[0] > 16 * half + 16:
                continue
            q_of = first + iota((16, 128), 1) // 32
            c_in = 6 * m + q_of
            j_of = c_in - (16 * half + iota((16, 128), 0)) + 1
            j_of = jnp.where((q_of < STEP) & (c_in < WA), j_of, -1)
            for k in range(3):
                for l in range(3):
                    for ra in range(2):
                        block = jnp.zeros((16, 128), F32)
                        for j in range(3):
                            t0 = ((1 - ra) * 3 + j) * 3 + k
                            t1 = ((2 - ra) * 3 + j) * 3 + k
                            value = jnp.where(
                                odd1,
                                spread[8 * t1 + l : 8 * t1 + l + 1, :],
                                spread[8 * t0 + l : 8 * t0 + l + 1, :],
                            )
                            block = jnp.where(j_of == j, value, block)
                        at = 64 * l + 32 * ra + 16 * half
                        w3[k, at : at + 16, 128 * tile : 128 * tile + 128] = block.astype(BF16)

    take = (iota((16, 128), 1) % 16 == iota((16, 128), 0)).astype(F32).astype(BF16)
    spread[...] = nn(wm_ref[...].reshape(81 * 16, 16), take)
    odd = (iota((16, 128), 1) // 16) % 2 == 1
    p_of = iota((16, 128), 1) // 32
    for k in range(3):
        for l in range(3):
            w2[3 * k + l, 192:256, :] = jnp.zeros((64, 256), BF16)
            for ra in range(2):
                values = []
                for j in range(3):
                    t0 = (((1 - ra) * 3 + j) * 3 + k) * 3 + l
                    t1 = (((2 - ra) * 3 + j) * 3 + k) * 3 + l
                    values.append(
                        jnp.where(odd, spread[16 * t1 : 16 * t1 + 16, :], spread[16 * t0 : 16 * t0 + 16, :])
                    )
                for q in range(STEP):
                    for tile in range(2):
                        block = jnp.zeros((16, 128), F32)
                        for j in range(3):
                            block = jnp.where(p_of == q + j - 4 * tile, values[j], block)
                        at = 32 * q + 16 * ra
                        w2[3 * k + l, at : at + 16, 128 * tile : 128 * tile + 128] = block.astype(BF16)


def shifted(values, by, edge):
    rows = values.shape[0]
    moved = pltpu.roll(values, by % rows, 0)
    return jnp.where(iota(values.shape, 0) % WB == edge, 0.0, moved)


def score_kernel(
    valid_ref, bf_ref, bm_ref, bl_ref, u_ref, own_ref, oth_ref, e_ref, wf_ref, wm_ref, wl_ref,
    out_ref, tmp, spread, w1, w2, w3, vbuf, xbuf, h1, h2,
):
    rank = lax.axis_index("trow")
    prepare(wf_ref, wm_ref, wl_ref, tmp, spread, w1, w2, w3)
    b1 = bias_row(bf_ref, 256)
    b2 = bias_row(bm_ref, 32 * STEP)

    own = own_ref[0]
    oth = oth_ref[...]
    u_own = u_ref[rank]
    u_oth = u_ref[1 - rank]
    raw = nt(own, jnp.concatenate([u_own] * 4, axis=0)) + nt(oth, jnp.concatenate([u_oth] * 4, axis=0))
    own32 = own.astype(F32)
    oth32 = oth.astype(F32)
    squares = jnp.sum(own32 * own32 + oth32 * oth32, axis=1, keepdims=True)
    live = iota((NB, 1), 0) // WB < valid_ref[0]
    corr = jnp.where(live, math.sqrt(1024) * raw * lax.rsqrt(squares + EPS_NORM), 0.0)
    magnitude = jnp.abs(corr)
    peak_query = jnp.max(magnitude, axis=1, keepdims=True)
    peak_target = jnp.max(magnitude, axis=0, keepdims=True)
    volume = corr * (corr * (1.0 / (peak_query + EPS_PEAK))) * (corr * (1.0 / (peak_target + EPS_PEAK)))
    lane = iota((NB, 256), 1)
    chosen = jnp.where(
        lane < 64, shifted(volume, 1, 0), jnp.where(lane < 128, volume, shifted(volume, -1, WB - 1))
    )
    vbuf[0:WB, :] = jnp.zeros((WB, 256), BF16)
    vbuf[WB + NB : 2 * WB + NB, :] = jnp.zeros((WB, 256), BF16)
    vbuf[WB : WB + NB, :] = chosen.astype(BF16)
    start = pl.multiple_of(rank * (6 * WB), 6 * WB)
    xbuf[...] = nn(vbuf[pl.ds(start, 12 * WB), :], e_ref[...]).astype(BF16)

    pad = pl.multiple_of((1 - rank) * WB, WB)

    lane = iota((10 * WB, 256), 1)
    for m in range(BLOCKS):
        acc = nn(xbuf[0 : 10 * WB, 128 * m : 128 * m + 128], w1[0])
        for k in (1, 2):
            acc = acc + nn(xbuf[WB * k : WB * k + 10 * WB, 128 * m : 128 * m + 128], w1[k])
        hidden = jnp.maximum(acc + b1, 0.0)
        if m == 0:
            hidden = jnp.where(lane < 32, 0.0, hidden)
        if m == BLOCKS - 1:
            hidden = jnp.where(lane >= 32 * (WA - 6 * m + 1), 0.0, hidden)
        zero = jnp.zeros((WB, 256), BF16)
        edge = pl.multiple_of(rank * (10 * WB), WB)
        for l in range(3):
            h1[m, l, pl.ds(edge, WB), :] = zero
        h1[m, 0, pl.ds(pad, 10 * WB), :] = shifted(hidden, 1, 0).astype(BF16)
        h1[m, 1, pl.ds(pad, 10 * WB), :] = hidden.astype(BF16)
        h1[m, 2, pl.ds(pad, 10 * WB), :] = shifted(hidden, -1, WB - 1).astype(BF16)

    edge = pl.multiple_of(rank * (9 * WB), WB)
    for m in range(BLOCKS):
        acc = jnp.zeros((9 * WB, 256), F32)
        for k in range(3):
            for l in range(3):
                acc = acc + nt(h1[m, l, WB * k : WB * k + 9 * WB, :], w2[3 * k + l])
        hidden = jnp.maximum(acc + b2, 0.0)
        h2[pl.ds(edge, WB), 256 * m : 256 * m + 256] = jnp.zeros((WB, 256), BF16)
        h2[pl.ds(pad, 9 * WB), 256 * m : 256 * m + 256] = hidden.astype(BF16)

    acc = nt(w3[0], h2[0 : 8 * WB, :])
    for k in (1, 2):
        acc = acc + nt(w3[k], h2[WB * k : WB * k + 8 * WB, :])
    column = iota((NA, 8 * WB), 1) % WB
    result = acc[NA : 2 * NA]
    result = result + jnp.where(column == 0, 0.0, pltpu.roll(acc[0:NA], 1, 1))
    result = result + jnp.where(column == WB - 1, 0.0, pltpu.roll(acc[2 * NA : 3 * NA], 8 * WB - 1, 1))
    result = result + bl_ref[0]
    row = rank * 8 + iota((NA, 8 * WB), 1) // WB
    out_ref[0] = jnp.where(row < valid_ref[0], result, 0.0)


def copy_matrix():
    source = jnp.arange(256, dtype=jnp.int32)[:, None]
    lane = jnp.arange(768, dtype=jnp.int32)[None, :]
    block, shift, inner = lane // 128, (lane // 32) % 4, lane % 32
    column, ref_row = 6 * block - 2 + inner // 2, inner % 2
    used = (inner < 20) & (column >= 0) & (column < WA) & (shift < 3)
    return (used & (source == shift * 64 + ref_row * WA + column)).astype(BF16)


def score(valid, b_first, b_middle, b_last, unit, own, other, wf, wm, wl):
    smem = pl.BlockSpec(memory_space=pltpu.SMEM)
    vmem = pl.BlockSpec(memory_space=pltpu.VMEM)
    return pl.pallas_call(
        score_kernel,
        out_shape=jax.ShapeDtypeStruct((1, NA, 8 * WB), F32),
        in_specs=[smem] * 4 + [vmem] * 7,
        out_specs=vmem,
        scratch_shapes=[
            pltpu.VMEM((27, 8, 128), F32),
            pltpu.VMEM((81 * 16, 128), F32),
            pltpu.VMEM((3, 128, 256), BF16),
            pltpu.VMEM((9, 256, 256), BF16),
            pltpu.VMEM((3, 192, 1536), BF16),
            pltpu.VMEM((NB + 2 * WB, 256), BF16),
            pltpu.VMEM((12 * WB, 768), BF16),
            pltpu.VMEM((BLOCKS, 3, 11 * WB, 256), BF16),
            pltpu.VMEM((10 * WB, 1536), BF16),
        ],
        compiler_params=pltpu.CompilerParams(vmem_limit_bytes=48 * 1024 * 1024),
        name="pair_scores",
    )(valid, b_first, b_middle, b_last, unit, own, other, copy_matrix(), wf, wm, wl)


def per_device(
    query_bank, ref_owner, target_feat, valid_rows, w_first, b_first, w_middle, b_middle, w_last, b_last
):
    n = lax.axis_size("pair")
    unit, other = exchange(ref_owner, query_bank, target_feat, n)
    wf = jnp.transpose(w_first, (1, 2, 3, 4, 5, 0)).reshape(27, 3, 16)
    wl = jnp.transpose(w_last, (0, 2, 3, 4, 5, 1)).reshape(27, 3, 16)
    wm = jnp.transpose(w_middle, (2, 3, 4, 5, 0, 1)).reshape(81, 16, 16)
    return score(valid_rows, b_first, b_middle, b_last, unit, target_feat, other, wf, wm, wl)


def solution(mesh):
    in_specs = (
        P("pair", None, None),
        P(),
        P("pair", None, "trow"),
        P("pair"),
        P(),
        P(),
        P(),
        P(),
        P(),
        P(),
    )
    out_specs = P("pair", None, "trow")
    return jax.shard_map(
        per_device, mesh=mesh, in_specs=in_specs, out_specs=out_specs, check_vma=False
    )
```

time: 1040 us -> 53 us (0.05)
  waiting for transfers between devices: 954 us -> 0 us
  Pallas kernels: 0 us -> 48 us
  other arithmetic: 18.8 us -> 0.15 us
  starting transfers between devices: 16.5 us -> 0 us
  local copies, waits for them, and re-layouts: 19 us -> 2.59 us
  between operations: 15.7 us -> 2.05 us
    psum x1 -> x0, waiting for transfers between devices: 936 us -> none  [broadcast(): return lax.psum(jnp.where(mine, shard, jnp.zeros_like(shard)), axis)]
    pallas_call x0 -> x2, Pallas kernels: none -> 48 us  [the longest x1 40.5 us: exchange(): pl.pallas_call(functools.partial(comm_kernel, n, places), out_shape=(jax....]
    ppermute x6 -> x0, waiting for transfers between devices: 17.8 us -> none  [the longest x3 15.2 us: extended(): lax.ppermute(head, axis, [((i + 1) % count, i) for i in range(ends)])]
    ppermute x6 -> x0, starting transfers between devices: 11.5 us -> none  [the longest x3 7.49 us: extended(): lax.ppermute(tail, axis, [(i, (i + 1) % count) for i in range(ends)])]
  transfers between devices with their start and end apart: 8 -> 0, of which waited for: 6 -> 0; matrix products, arithmetic and copies ran while one was open for 1% -> 0% of each run, Pallas kernels for 0% -> 0%
where the time goes in v1:
time: 53 us; the launch traced here: 52.8 us
  Pallas kernels  48 us (91%)
  local copies, waits for them, and re-layouts  2.59 us (5%)
  between operations  2.05 us (4%)
    pallas_call x1, Pallas kernels, exchange(): pl.pallas_call(functools.partial(comm_kernel, n, places), out_shape=(jax....  40.5 us
    pallas_call x1, Pallas kernels, score(): pl.pallas_call(score_kernel, out_shape=jax.ShapeDtypeStruct((1, NA, 8 * W...  7.5 us
    unnamed x16, local copies, waits for them, and re-layouts  2.59 us

profile of v1, /device:TPU:1, one launch (start us, length us, event | category | flops | bytes accessed | tf_op | source)
XLA Modules:
  0.0 52.8 jit_solution(6759688965033566973)
XLA Ops:
  2.0 0.0 copy-start
  2.0 0.1 fusion.1.e_ref
  2.1 0.0 copy-start.2
  2.1 0.0 copy-start.4
  2.2 0.0 copy-start.5
  2.2 40.5 %window_exchange.1 = (bf16[2,64,512]{2,1,0:T(8,128)(2,1)}, bf16[512,512]{1,0:T(8,128)(2,1)}) custom-call(s32[1]{0:T(128)S(6)} %copy.11.owner_ref, bf16[1,64,1024]{2,1,0:T(8,128)(2,1)} %q_ref.1, bf16[1,512,512]{2,1,0:T(8,128)(2,1)} %own_ref.1), custom_call_target="tpu_custom_call" | custom-call | tf_op jit(solution)/shard_map/window_exchange/pallas_call | solution.py:171
  42.7 0.0 copy-start.6
  42.7 0.0 copy-start.7
  42.7 0.0 copy-done
  42.7 0.0 copy-done.2
  42.7 0.0 copy-done.4
  42.7 0.0 copy-done.5
  42.7 0.6 %copy-done.6 = f32[16]{0:T(128)S(1)} copy-done((f32[16]{0:T(128)S(1)}, f32[16]{0:T(128)}, u32[]{:S(2)}) %copy-start.6) | copy-done | bytes 88
  43.3 0.0 copy-done.7
  43.3 0.0 copy-start.1
  43.4 1.0 %copy-done.1 = bf16[512,512]{1,0:T(8,128)(2,1)S(1)} copy-done((bf16[512,512]{1,0:T(8,128)(2,1)S(1)}, bf16[512,512]{1,0:T(8,128)(2,1)}, u32[]{:S(2)}) %copy-start.1) | copy-done | bytes 524312
  44.4 0.0 copy-start.3
  44.4 0.9 %copy-done.3 = bf16[2,64,512]{2,1,0:T(8,128)(2,1)S(1)} copy-done((bf16[2,64,512]{2,1,0:T(8,128)(2,1)S(1)}, bf16[2,64,512]{2,1,0:T(8,128)(2,1)}, u32[]{:S(2)}) %copy-start.3) | copy-done | bytes 131096
  45.3 7.5 %pair_scores.1 = f32[1,64,256]{2,1,0:T(8,128)} custom-call(s32[1]{0:T(128)S(6)} %copy.12.valid_ref, f32[16]{0:T(128)S(1)} %copy-done.6, f32[16]{0:T(128)S(1)} %copy-done.7, f32[1]{0:T(128)S(6)} %copy.13.bl_ref, bf16[2,64,512]{2,1,0:T(8,128)(2,1)S(1)} %copy-done.3, bf16[1,512,512]{2,1,0:T(8,128)(2,1)S(1)} %copy-done, bf16[512,512]{1,0:T(8,128)(2,1)S(1)} %copy-done.1, ...), custom_call_target="tpu_custom_call" | custom-call | tf_op jit(solution)/shard_map/pair_scores/pallas_call | solution.py:380
  (2 shorter events, 0.0 us)
Async XLA Ops:
  2.0 40.7 %copy-start = (bf16[1,512,512]{2,1,0:T(8,128)(2,1)S(1)}, bf16[1,512,512]{2,1,0:T(8,128)(2,1)}, u32[]{:S(2)}) copy-start(bf16[1,512,512]{2,1,0:T(8,128)(2,1)} %own_ref.1) | copy-start | bytes 1572868
  2.1 40.6 %copy-start.2 = (bf16[16,16,3,3,3,3]{1,0,5,4,3,2:T(8,128)(2,1)S(1)}, bf16[16,16,3,3,3,3]{1,0,5,4,3,2:T(8,128)(2,1)}, u32[]{:S(2)}) copy-start(bf16[16,16,3,3,3,3]{1,0,5,4,3,2:T(8,128)(2,1)} %param.16) | copy-start | bytes 124420
  2.1 40.6 %copy-start.4 = (bf16[16,1,3,3,3,3]{0,5,4,3,2,1:T(4,128)(2,1)S(1)}, bf16[16,1,3,3,3,3]{0,5,4,3,2,1:T(4,128)(2,1)}, u32[]{:S(2)}) copy-start(bf16[16,1,3,3,3,3]{0,5,4,3,2,1:T(4,128)(2,1)} %param.14) | copy-start | bytes 7780
  2.2 40.6 %copy-start.5 = (bf16[1,16,3,3,3,3]{1,5,4,3,2,0:T(4,128)(2,1)S(1)}, bf16[1,16,3,3,3,3]{1,5,4,3,2,0:T(4,128)(2,1)}, u32[]{:S(2)}) copy-start(bf16[1,16,3,3,3,3]{1,5,4,3,2,0:T(4,128)(2,1)} %param.18) | copy-start | bytes 7780
  42.7 0.7 %copy-start.6 = (f32[16]{0:T(128)S(1)}, f32[16]{0:T(128)}, u32[]{:S(2)}) copy-start(f32[16]{0:T(128)} %bf_ref.1) | copy-start | bytes 196
  42.7 0.7 %copy-start.7 = (f32[16]{0:T(128)S(1)}, f32[16]{0:T(128)}, u32[]{:S(2)}) copy-start(f32[16]{0:T(128)} %bm_ref.1) | copy-start | bytes 196
  43.3 1.0 %copy-start.1 = (bf16[512,512]{1,0:T(8,128)(2,1)S(1)}, bf16[512,512]{1,0:T(8,128)(2,1)}, u32[]{:S(2)}) copy-start(bf16[512,512]{1,0:T(8,128)(2,1)} %get-tuple-element.8.oth_ref) | copy-start | bytes 1572868
  44.4 0.9 %copy-start.3 = (bf16[2,64,512]{2,1,0:T(8,128)(2,1)S(1)}, bf16[2,64,512]{2,1,0:T(8,128)(2,1)}, u32[]{:S(2)}) copy-start(bf16[2,64,512]{2,1,0:T(8,128)(2,1)} %get-tuple-element.7.u_ref) | copy-start | bytes 393220

commit v2 on v1

v2 whole, which is shorter than its diff:
```python
import functools
import math

import jax
import jax.numpy as jnp
from jax import lax
from jax.experimental import pallas as pl
from jax.experimental.pallas import tpu as pltpu
from jax.sharding import PartitionSpec as P

MESH = pl.DeviceIdType.MESH
WB = 32
WA = 32
HB = 16
NB = HB * WB
NA = 64
EPS_NORM = 1e-06
EPS_PEAK = 1e-05
F32 = jnp.float32
BF16 = jnp.bfloat16

BLOCKS = 6
STEP = 6
HALF = 512


def nt(left, right):
    return lax.dot_general(left, right, (((1,), (1,)), ((), ())), preferred_element_type=F32)


def nn(left, right):
    return lax.dot_general(left, right, (((1,), (0,)), ((), ())), preferred_element_type=F32)


def iota(shape, dim):
    return lax.broadcasted_iota(jnp.int32, shape, dim)


def spread_rows(src_ref, tmp):
    tmp[...] = jnp.zeros_like(tmp)
    for t in range(27):
        tmp[t, 0:3, 0:16] = src_ref[t].astype(F32)
    flat = tmp[...].reshape(216, 128).astype(BF16)
    take = (iota((128, 128), 1) % 16 == iota((128, 128), 0)).astype(F32).astype(BF16)
    return nn(flat, take)


def bias_row(b_ref, used):
    lane = iota((1, 256), 1)
    row = jnp.zeros((1, 256), F32)
    for o in range(16):
        row = jnp.where(lane % 16 == o, b_ref[o], row)
    return jnp.where(lane < used, row, 0.0)


def prepare(wf_ref, wm_ref, wl_ref, tmp, spread, w1, w2, w3):
    spread[0:216, :] = spread_rows(wf_ref, tmp)
    row = iota((32, 128), 0)
    lane = iota((32, 128), 1)
    for tile in range(2):
        j_of = row // 2 - (tile * 4 + lane // 32)
        i_of = row % 2 - (lane // 16) % 2 + 1
        for k in range(3):
            for l in range(4):
                block = jnp.zeros((32, 128), F32)
                if l < 3:
                    for i in range(3):
                        for j in range(3):
                            t = (i * 3 + j) * 3 + k
                            value = spread[8 * t + l : 8 * t + l + 1, :]
                            block = jnp.where((j_of == j) & (i_of == i), value, block)
                w1[k, 32 * l : 32 * l + 32, 128 * tile : 128 * tile + 128] = block.astype(BF16)

    spread[0:216, :] = spread_rows(wl_ref, tmp)
    w3[...] = jnp.zeros_like(w3)
    odd1 = (iota((1, 128), 1) // 16) % 2 == 1
    for half in range(2):
        for tile in range(12):
            m, first = tile // 2, (tile % 2) * 4
            columns = [6 * m + q for q in range(first, first + 4) if q < STEP and 6 * m + q < WA]
            if not columns or columns[-1] < 16 * half - 1 or columns[0] > 16 * half + 16:
                continue
            q_of = first + iota((16, 128), 1) // 32
            c_in = 6 * m + q_of
            j_of = c_in - (16 * half + iota((16, 128), 0)) + 1
            j_of = jnp.where((q_of < STEP) & (c_in < WA), j_of, -1)
            for k in range(3):
                for l in range(3):
                    for ra in range(2):
                        block = jnp.zeros((16, 128), F32)
                        for j in range(3):
                            t0 = ((1 - ra) * 3 + j) * 3 + k
                            t1 = ((2 - ra) * 3 + j) * 3 + k
                            value = jnp.where(
                                odd1,
                                spread[8 * t1 + l : 8 * t1 + l + 1, :],
                                spread[8 * t0 + l : 8 * t0 + l + 1, :],
                            )
                            block = jnp.where(j_of == j, value, block)
                        at = 64 * l + 32 * ra + 16 * half
                        w3[k, at : at + 16, 128 * tile : 128 * tile + 128] = block.astype(BF16)

    take = (iota((16, 128), 1) % 16 == iota((16, 128), 0)).astype(F32).astype(BF16)
    spread[...] = nn(wm_ref[...].reshape(81 * 16, 16), take)
    odd = (iota((16, 128), 1) // 16) % 2 == 1
    p_of = iota((16, 128), 1) // 32
    for k in range(3):
        for l in range(3):
            w2[3 * k + l, 192:256, :] = jnp.zeros((64, 256), BF16)
            for ra in range(2):
                values = []
                for j in range(3):
                    t0 = (((1 - ra) * 3 + j) * 3 + k) * 3 + l
                    t1 = (((2 - ra) * 3 + j) * 3 + k) * 3 + l
                    values.append(
                        jnp.where(odd, spread[16 * t1 : 16 * t1 + 16, :], spread[16 * t0 : 16 * t0 + 16, :])
                    )
                for q in range(STEP):
                    for tile in range(2):
                        block = jnp.zeros((16, 128), F32)
                        for j in range(3):
                            block = jnp.where(p_of == q + j - 4 * tile, values[j], block)
                        at = 32 * q + 16 * ra
                        w2[3 * k + l, at : at + 16, 128 * tile : 128 * tile + 128] = block.astype(BF16)


def shifted(values, by, edge):
    rows = values.shape[0]
    moved = pltpu.roll(values, by % rows, 0)
    return jnp.where(iota(values.shape, 0) % WB == edge, 0.0, moved)


def copy_matrix(e_ref):
    for m in range(BLOCKS):
        source = iota((256, 128), 0)
        lane = iota((256, 128), 1)
        shift, inner = lane // 32, lane % 32
        column, ref_row = 6 * m - 2 + inner // 2, inner % 2
        used = (inner < 20) & (column >= 0) & (column < WA) & (shift < 3)
        hit = used & (source == shift * NA + ref_row * WA + column)
        e_ref[:, 128 * m : 128 * m + 128] = jnp.where(hit, 1.0, 0.0).astype(BF16)


def unit_slices(values, unit, plane, rows):
    values = values.astype(F32)
    scale = lax.rsqrt(jnp.sum(values * values, axis=1, keepdims=True) + EPS_NORM)
    normed = values * scale
    mine = jnp.where(plane == 0, normed[:, 0:HALF], normed[:, HALF : 2 * HALF])
    for s in range(32):
        g, t = s // 4, s % 4
        at = 8 * s
        unit[at // rows, at % rows : at % rows + 8, :] = mine[8 * g : 8 * g + 8, 128 * t : 128 * t + 128].astype(BF16)


def squares_of(feats, out_ref):
    values = feats.astype(F32)
    sums = jnp.sum(values * values, axis=1, keepdims=True)
    for t in range(4):
        wide = jnp.broadcast_to(sums[128 * t : 128 * t + 128], (128, 128))
        out_ref[t : t + 1, :] = jnp.transpose(wide)[0:1, :]


def kernel(
    sizes, owner_ref, valid_ref, bf_ref, bm_ref, bl_ref, q_hbm, t_hbm, wf_hbm, wm_hbm, wl_hbm,
    out_ref,
    q_ref, t_ref, wf_ref, wm_ref, wl_ref, unit, recv_a, cand, recv_b, piece, gath, sq_own, sq_oth, part, part_oth,
    tmp, spread, w1, w2, w3, e_ref, vbuf, xbuf, h1, h2, loads, sems,
):
    group, depth, inner, rows = sizes
    me = lax.axis_index("pair")
    plane = lax.axis_index("trow")
    z = lax.rem(me // inner, depth)
    g = (me // (inner * depth)) * inner + lax.rem(me, inner)

    def at(g_of, z_of):
        return ((g_of // inner) * depth + z_of) * inner + lax.rem(g_of, inner)

    def in_group(o):
        return at(lax.rem(g + o, group), z)

    def along(o):
        return at(g, lax.rem(z + o, depth))

    barrier = pltpu.get_barrier_semaphore()

    def greet(pair, trow):
        pl.semaphore_signal(barrier, inc=1, device_id=(pair, trow), device_id_type=MESH)

    pl.loop(1, depth)(lambda o: greet(along(o), plane))
    if group > 1:
        pl.loop(1, group)(lambda o: greet(in_group(o), plane))
    greet(me, 1 - plane)

    local = [
        pltpu.make_async_copy(src, dst, loads.at[i])
        for i, (src, dst) in enumerate(
            ((q_hbm.at[0], q_ref), (wf_hbm, wf_ref), (wl_hbm, wl_ref), (wm_hbm, wm_ref), (t_hbm.at[0], t_ref))
        )
    ]
    for copy in local:
        copy.start()
    copy_matrix(e_ref)
    local[0].wait()
    unit_slices(q_ref[...], unit, plane, rows)
    for copy in local[1:4]:
        copy.wait()
    prepare(wf_ref, wm_ref, wl_ref, tmp, spread, w1, w2, w3)
    local[4].wait()
    squares_of(t_ref[...], sq_own)

    pl.semaphore_wait(barrier, (depth - 1) + (group - 1) + 1)

    def send(src, dst, k, pair, trow):
        copy = pltpu.make_async_remote_copy(
            src_ref=src,
            dst_ref=dst,
            send_sem=sems.at[2 * k],
            recv_sem=sems.at[2 * k + 1],
            device_id=(pair, trow),
            device_id_type=MESH,
        )
        copy.start()
        return copy

    def wait(ref, k):
        pltpu.make_async_copy(ref, ref, sems.at[k]).wait()

    owner = owner_ref[0]
    owner_g = (owner // (inner * depth)) * inner + lax.rem(owner, inner)
    owner_z = lax.rem(owner // inner, depth)

    if group > 1:
        pl.loop(1, group)(
            lambda o: send(unit.at[lax.rem(g + o, group)], recv_a.at[g], 0, in_group(o), plane) and None
        )
    squares = send(sq_own, sq_oth, 4, me, 1 - plane)
    recv_a[g] = unit[g]
    if group > 1:
        wait(recv_a.at[pl.ds(0, group - 1)], 1)
    chosen = recv_a[owner_g]
    cand[...] = chosen
    recv_b[z] = chosen

    pl.loop(1, depth)(lambda o: send(cand, recv_b.at[z], 1, along(o), plane) and None)
    wait(recv_b.at[pl.ds(0, depth - 1)], 3)
    chosen = recv_b[owner_z]
    piece[...] = chosen
    gath[g] = chosen

    if group > 1:
        pl.loop(1, group)(lambda o: send(piece, gath.at[g], 2, in_group(o), plane) and None)
        wait(gath.at[pl.ds(0, group - 1)], 5)
    lines = []
    for line in range(8):
        tiles = []
        for t in range(4):
            first = 8 * (4 * line + t)
            tiles.append(gath[first // rows, first % rows : first % rows + 8, :].astype(F32))
        lines.append(jnp.concatenate(tiles, axis=1))
    window = jnp.concatenate(lines, axis=0).astype(BF16)

    blank = jnp.zeros((NA, HALF), BF16)
    part[...] = nt(t_ref[0:256, :], jnp.concatenate([window, blank], axis=0)) + nt(
        t_ref[256:512, :], jnp.concatenate([blank, window], axis=0)
    )
    partial = send(part, part_oth, 3, me, 1 - plane)

    b1 = bias_row(bf_ref, 256)
    b2 = bias_row(bm_ref, 32 * STEP)
    squares.wait()
    columns = []
    for t in range(4):
        total = sq_own[t : t + 1, :] + sq_oth[t : t + 1, :]
        columns.append(jnp.transpose(jnp.broadcast_to(total, (128, 128))))
    inverse = lax.rsqrt(jnp.concatenate(columns, axis=0) + EPS_NORM)
    live = iota((NB, 128), 0) // WB < valid_ref[0]

    partial.wait()
    both = part[...] + part_oth[...]
    swapped = pltpu.roll(both, 64, 1)
    low = iota((256, 128), 1) < 64
    raw = jnp.concatenate([jnp.where(low, both, swapped), jnp.where(low, swapped, both)], axis=0)
    corr = jnp.where(live, math.sqrt(1024) * raw * inverse, 0.0)
    magnitude = jnp.abs(corr)
    peak_query = jnp.max(magnitude, axis=1, keepdims=True)
    peak_target = jnp.max(magnitude, axis=0, keepdims=True)
    volume = corr * (corr * (1.0 / (peak_query + EPS_PEAK))) * (corr * (1.0 / (peak_target + EPS_PEAK)))
    vbuf[0:WB, :] = jnp.zeros((WB, 256), BF16)
    vbuf[WB + NB : 2 * WB + NB, :] = jnp.zeros((WB, 256), BF16)
    low = iota((NB, 128), 1) < 64
    vbuf[WB : WB + NB, 0:128] = jnp.where(low, shifted(volume, 1, 0), volume).astype(BF16)
    vbuf[WB : WB + NB, 128:256] = shifted(volume, -1, WB - 1).astype(BF16)
    start = pl.multiple_of(plane * (6 * WB), 6 * WB)
    xbuf[...] = nn(vbuf[pl.ds(start, 12 * WB), :], e_ref[...]).astype(BF16)

    pad = pl.multiple_of((1 - plane) * WB, WB)

    lane = iota((10 * WB, 256), 1)
    for m in range(BLOCKS):
        acc = nn(xbuf[0 : 10 * WB, 128 * m : 128 * m + 128], w1[0])
        for k in (1, 2):
            acc = acc + nn(xbuf[WB * k : WB * k + 10 * WB, 128 * m : 128 * m + 128], w1[k])
        hidden = jnp.maximum(acc + b1, 0.0)
        if m == 0:
            hidden = jnp.where(lane < 32, 0.0, hidden)
        if m == BLOCKS - 1:
            hidden = jnp.where(lane >= 32 * (WA - 6 * m + 1), 0.0, hidden)
        zero = jnp.zeros((WB, 256), BF16)
        edge = pl.multiple_of(plane * (10 * WB), WB)
        for l in range(3):
            h1[m, l, pl.ds(edge, WB), :] = zero
        h1[m, 0, pl.ds(pad, 10 * WB), :] = shifted(hidden, 1, 0).astype(BF16)
        h1[m, 1, pl.ds(pad, 10 * WB), :] = hidden.astype(BF16)
        h1[m, 2, pl.ds(pad, 10 * WB), :] = shifted(hidden, -1, WB - 1).astype(BF16)

    edge = pl.multiple_of(plane * (9 * WB), WB)
    for m in range(BLOCKS):
        acc = jnp.zeros((9 * WB, 256), F32)
        for k in range(3):
            for l in range(3):
                acc = acc + nt(h1[m, l, WB * k : WB * k + 9 * WB, :], w2[3 * k + l])
        hidden = jnp.maximum(acc + b2, 0.0)
        h2[pl.ds(edge, WB), 256 * m : 256 * m + 256] = jnp.zeros((WB, 256), BF16)
        h2[pl.ds(pad, 9 * WB), 256 * m : 256 * m + 256] = hidden.astype(BF16)

    acc = nt(w3[0], h2[0 : 8 * WB, :])
    for k in (1, 2):
        acc = acc + nt(w3[k], h2[WB * k : WB * k + 8 * WB, :])
    column = iota((NA, 8 * WB), 1) % WB
    result = acc[NA : 2 * NA]
    result = result + jnp.where(column == 0, 0.0, pltpu.roll(acc[0:NA], 1, 1))
    result = result + jnp.where(column == WB - 1, 0.0, pltpu.roll(acc[2 * NA : 3 * NA], 8 * WB - 1, 1))
    result = result + bl_ref[0]
    row = plane * 8 + iota((NA, 8 * WB), 1) // WB
    out_ref[0] = jnp.where(row < valid_ref[0], result, 0.0)

    if group > 1:
        wait(recv_a.at[pl.ds(0, group - 1)], 0)
        wait(gath.at[pl.ds(0, group - 1)], 4)
    wait(recv_b.at[pl.ds(0, depth - 1)], 2)


def layout_of(n):
    inner = min(8, max(1, n // 2))
    depth = min(8, n // inner)
    group = n // depth
    return group, depth, inner, 256 // group


def score(owner, valid, b_first, b_middle, b_last, bank, feats, wf, wm, wl, n):
    smem = pl.BlockSpec(memory_space=pltpu.SMEM)
    hbm = pl.BlockSpec(memory_space=pltpu.HBM)
    sizes = layout_of(n)
    group, depth, _, rows = sizes
    return pl.pallas_call(
        functools.partial(kernel, sizes),
        out_shape=jax.ShapeDtypeStruct((1, NA, 8 * WB), F32),
        in_specs=[smem] * 5 + [hbm] * 5,
        out_specs=pl.BlockSpec(memory_space=pltpu.VMEM),
        scratch_shapes=[
            pltpu.VMEM((NA, 2 * HALF), BF16),
            pltpu.VMEM((NB, HALF), BF16),
            pltpu.VMEM((27, 3, 16), BF16),
            pltpu.VMEM((81, 16, 16), BF16),
            pltpu.VMEM((27, 3, 16), BF16),
            pltpu.VMEM((group, rows, 128), BF16),
            pltpu.VMEM((group, rows, 128), BF16),
            pltpu.VMEM((rows, 128), BF16),
            pltpu.VMEM((depth, rows, 128), BF16),
            pltpu.VMEM((rows, 128), BF16),
            pltpu.VMEM((group, rows, 128), BF16),
            pltpu.VMEM((8, 128), F32),
            pltpu.VMEM((8, 128), F32),
            pltpu.VMEM((256, 128), F32),
            pltpu.VMEM((256, 128), F32),
            pltpu.VMEM((27, 8, 128), F32),
            pltpu.VMEM((81 * 16, 128), F32),
            pltpu.VMEM((3, 128, 256), BF16),
            pltpu.VMEM((9, 256, 256), BF16),
            pltpu.VMEM((3, 192, 1536), BF16),
            pltpu.VMEM((256, 768), BF16),
            pltpu.VMEM((NB + 2 * WB, 256), BF16),
            pltpu.VMEM((12 * WB, 768), BF16),
            pltpu.VMEM((BLOCKS, 3, 11 * WB, 256), BF16),
            pltpu.VMEM((10 * WB, 1536), BF16),
            pltpu.SemaphoreType.DMA((5,)),
            pltpu.SemaphoreType.DMA((10,)),
        ],
        compiler_params=pltpu.CompilerParams(
            collective_id=0, has_side_effects=True, vmem_limit_bytes=48 * 1024 * 1024
        ),
        name="pair_scores",
    )(owner, valid, b_first, b_middle, b_last, bank, feats, wf, wm, wl)


def per_device(
    query_bank, ref_owner, target_feat, valid_rows, w_first, b_first, w_middle, b_middle, w_last, b_last
):
    wf = jnp.transpose(w_first, (1, 2, 3, 4, 5, 0)).reshape(27, 3, 16)
    wl = jnp.transpose(w_last, (0, 2, 3, 4, 5, 1)).reshape(27, 3, 16)
    wm = jnp.transpose(w_middle, (2, 3, 4, 5, 0, 1)).reshape(81, 16, 16)
    n = lax.axis_size("pair")
    return score(ref_owner, valid_rows, b_first, b_middle, b_last, query_bank, target_feat, wf, wm, wl, n)


def solution(mesh):
    in_specs = (
        P("pair", None, None),
        P(),
        P("pair", None, "trow"),
        P("pair"),
        P(),
        P(),
        P(),
        P(),
        P(),
        P(),
    )
    out_specs = P("pair", None, "trow")
    return jax.shard_map(
        per_device, mesh=mesh, in_specs=in_specs, out_specs=out_specs, check_vma=False
    )
```

time: 53 us -> 42.4 us (0.80)
  Pallas kernels: 48 us -> 34.4 us
  local copies, waits for them, and re-layouts: 2.59 us -> 5.7 us
    pallas_call x2 -> x1, Pallas kernels: 48 us -> 34.4 us  [score(): pl.pallas_call(functools.partial(kernel, sizes), out_shape=jax.ShapeDtype...]
    unnamed x16 -> x15, local copies, waits for them, and re-layouts: 2.59 us -> 5.7 us
where the time goes in v2:
time: 42.4 us; the launch traced here: 42.1 us
  Pallas kernels  34.4 us (81%)
  local copies, waits for them, and re-layouts  5.7 us (13%)
  between operations  1.97 us (5%)
    pallas_call x1, Pallas kernels, score(): pl.pallas_call(functools.partial(kernel, sizes), out_shape=jax.ShapeDtype...  34.4 us
    unnamed x15, local copies, waits for them, and re-layouts  5.7 us

profile of v2, /device:TPU:1, one launch (start us, length us, event | category | flops | bytes accessed | tf_op | source)
XLA Modules:
  0.0 42.1 jit_solution(15841709063950185218)
XLA Ops:
  1.9 0.0 copy-start.5
  2.0 0.0 copy-start.6
  2.0 0.6 %copy-done.5 = f32[16]{0:T(128)S(1)} copy-done((f32[16]{0:T(128)S(1)}, f32[16]{0:T(128)}, u32[]{:S(2)}) %copy-start.5) | copy-done | bytes 88
  2.6 0.0 copy-done.6
  2.6 0.0 copy-start
  2.6 1.0 %copy-done = bf16[1,512,512]{2,1,0:T(8,128)(2,1)S(1)} copy-done((bf16[1,512,512]{2,1,0:T(8,128)(2,1)S(1)}, bf16[1,512,512]{2,1,0:T(8,128)(2,1)}, u32[]{:S(2)}) %copy-start) | copy-done | bytes 524312
  3.7 0.0 copy-start.1
  3.7 1.0 %copy-done.1 = bf16[16,16,3,3,3,3]{1,0,5,4,3,2:T(8,128)(2,1)S(1)} copy-done((bf16[16,16,3,3,3,3]{1,0,5,4,3,2:T(8,128)(2,1)S(1)}, bf16[16,16,3,3,3,3]{1,0,5,4,3,2:T(8,128)(2,1)}, u32[]{:S(2)}) %copy-start.1) | copy-done | bytes 41496
  4.6 0.0 copy-start.2
  4.6 0.9 %copy-done.2 = bf16[1,64,1024]{2,1,0:T(8,128)(2,1)S(1)} copy-done((bf16[1,64,1024]{2,1,0:T(8,128)(2,1)S(1)}, bf16[1,64,1024]{2,1,0:T(8,128)(2,1)}, u32[]{:S(2)}) %copy-start.2) | copy-done | bytes 131096
  5.5 0.0 copy-start.3
  5.5 0.7 %copy-done.3 = bf16[16,1,3,3,3,3]{0,5,4,3,2,1:T(4,128)(2,1)S(1)} copy-done((bf16[16,1,3,3,3,3]{0,5,4,3,2,1:T(4,128)(2,1)S(1)}, bf16[16,1,3,3,3,3]{0,5,4,3,2,1:T(4,128)(2,1)}, u32[]{:S(2)}) %copy-start.3) | copy-done | bytes 2616
  6.3 0.0 copy-start.4
  6.3 0.7 %copy-done.4 = bf16[1,16,3,3,3,3]{1,5,4,3,2,0:T(4,128)(2,1)S(1)} copy-done((bf16[1,16,3,3,3,3]{1,5,4,3,2,0:T(4,128)(2,1)S(1)}, bf16[1,16,3,3,3,3]{1,5,4,3,2,0:T(4,128)(2,1)}, u32[]{:S(2)}) %copy-start.4) | copy-done | bytes 2616
  7.0 34.4 %pair_scores.1 = f32[1,64,256]{2,1,0:T(8,128)S(1)} custom-call(s32[1]{0:T(128)S(6)} %copy.12.owner_ref, s32[1]{0:T(128)S(6)} %copy.13.valid_ref, f32[16]{0:T(128)S(1)} %copy-done.5, f32[16]{0:T(128)S(1)} %copy-done.6, f32[1]{0:T(128)S(6)} %copy.14.bl_ref, bf16[1,64,1024]{2,1,0:T(8,128)(2,1)S(1)} %copy-done.2, bf16[1,512,512]{2,1,0:T(8,128)(2,1)S(1)} %copy-done, ...), custom_call_target="tpu_custom_call" | custom-call | tf_op jit(solution)/shard_map/pair_scores/pallas_call | solution.py:355
  41.4 0.6 %copy.15 = f32[1,64,256]{2,1,0:T(8,128)} copy(f32[1,64,256]{2,1,0:T(8,128)S(1)} %pair_scores.1) | data formatting | bytes 131072
Async XLA Ops:
  1.9 0.7 %copy-start.5 = (f32[16]{0:T(128)S(1)}, f32[16]{0:T(128)}, u32[]{:S(2)}) copy-start(f32[16]{0:T(128)} %bf_ref.1) | copy-start | bytes 196
  2.0 0.7 %copy-start.6 = (f32[16]{0:T(128)S(1)}, f32[16]{0:T(128)}, u32[]{:S(2)}) copy-start(f32[16]{0:T(128)} %bm_ref.1) | copy-start | bytes 196
  2.6 1.0 %copy-start = (bf16[1,512,512]{2,1,0:T(8,128)(2,1)S(1)}, bf16[1,512,512]{2,1,0:T(8,128)(2,1)}, u32[]{:S(2)}) copy-start(bf16[1,512,512]{2,1,0:T(8,128)(2,1)} %t_hbm.1) | copy-start | bytes 1572868
  3.7 1.0 %copy-start.1 = (bf16[16,16,3,3,3,3]{1,0,5,4,3,2:T(8,128)(2,1)S(1)}, bf16[16,16,3,3,3,3]{1,0,5,4,3,2:T(8,128)(2,1)}, u32[]{:S(2)}) copy-start(bf16[16,16,3,3,3,3]{1,0,5,4,3,2:T(8,128)(2,1)} %param.16) | copy-start | bytes 124420
  4.6 0.9 %copy-start.2 = (bf16[1,64,1024]{2,1,0:T(8,128)(2,1)S(1)}, bf16[1,64,1024]{2,1,0:T(8,128)(2,1)}, u32[]{:S(2)}) copy-start(bf16[1,64,1024]{2,1,0:T(8,128)(2,1)} %q_hbm.1) | copy-start | bytes 393220
  5.5 0.7 %copy-start.3 = (bf16[16,1,3,3,3,3]{0,5,4,3,2,1:T(4,128)(2,1)S(1)}, bf16[16,1,3,3,3,3]{0,5,4,3,2,1:T(4,128)(2,1)}, u32[]{:S(2)}) copy-start(bf16[16,1,3,3,3,3]{0,5,4,3,2,1:T(4,128)(2,1)} %param.14) | copy-start | bytes 7780
  6.3 0.7 %copy-start.4 = (bf16[1,16,3,3,3,3]{1,5,4,3,2,0:T(4,128)(2,1)S(1)}, bf16[1,16,3,3,3,3]{1,5,4,3,2,0:T(4,128)(2,1)}, u32[]{:S(2)}) copy-start(bf16[1,16,3,3,3,3]{1,5,4,3,2,0:T(4,128)(2,1)} %param.18) | copy-start | bytes 7780

commit v3 on v2

--- a/solution.py
+++ b/solution.py
@@ -161,9 +161,9 @@
 
 
 def kernel(
-    sizes, owner_ref, valid_ref, bf_ref, bm_ref, bl_ref, q_hbm, t_hbm, wf_hbm, wm_hbm, wl_hbm,
+    sizes, owner_hbm, valid_hbm, bf_hbm, bm_hbm, bl_hbm, q_hbm, t_hbm, wf_hbm, wm_hbm, wl_hbm,
     out_ref,
-    q_ref, t_ref, wf_ref, wm_ref, wl_ref, unit, recv_a, cand, recv_b, piece, gath, sq_own, sq_oth, part, part_oth,
+    owner_ref, valid_ref, bf_ref, bm_ref, bl_ref, q_ref, t_ref, wf_ref, wm_ref, wl_ref, unit, recv_a, cand, recv_b, piece, gath, sq_own, sq_oth, part, part_oth,
     tmp, spread, w1, w2, w3, e_ref, vbuf, xbuf, h1, h2, loads, sems,
 ):
     group, depth, inner, rows = sizes
@@ -194,7 +194,18 @@
     local = [
         pltpu.make_async_copy(src, dst, loads.at[i])
         for i, (src, dst) in enumerate(
-            ((q_hbm.at[0], q_ref), (wf_hbm, wf_ref), (wl_hbm, wl_ref), (wm_hbm, wm_ref), (t_hbm.at[0], t_ref))
+            (
+                (q_hbm.at[0], q_ref),
+                (wf_hbm, wf_ref),
+                (wl_hbm, wl_ref),
+                (wm_hbm, wm_ref),
+                (t_hbm.at[0], t_ref),
+                (owner_hbm, owner_ref),
+                (valid_hbm, valid_ref),
+                (bf_hbm, bf_ref),
+                (bm_hbm, bm_ref),
+                (bl_hbm, bl_ref),
+            )
         )
     ]
     for copy in local:
@@ -205,7 +216,8 @@
     for copy in local[1:4]:
         copy.wait()
     prepare(wf_ref, wm_ref, wl_ref, tmp, spread, w1, w2, w3)
-    local[4].wait()
+    for copy in local[4:]:
+        copy.wait()
     squares_of(t_ref[...], sq_own)
 
     pl.semaphore_wait(barrier, (depth - 1) + (group - 1) + 1)
@@ -348,16 +360,20 @@
 
 
 def score(owner, valid, b_first, b_middle, b_last, bank, feats, wf, wm, wl, n):
-    smem = pl.BlockSpec(memory_space=pltpu.SMEM)
     hbm = pl.BlockSpec(memory_space=pltpu.HBM)
     sizes = layout_of(n)
     group, depth, _, rows = sizes
     return pl.pallas_call(
         functools.partial(kernel, sizes),
-        out_shape=jax.ShapeDtypeStruct((1, NA, 8 * WB), F32),
-        in_specs=[smem] * 5 + [hbm] * 5,
+        out_shape=pltpu.VMEM((1, NA, 8 * WB), F32),
+        in_specs=[hbm] * 10,
         out_specs=pl.BlockSpec(memory_space=pltpu.VMEM),
         scratch_shapes=[
+            pltpu.SMEM((1,), jnp.int32),
+            pltpu.SMEM((1,), jnp.int32),
+            pltpu.SMEM((16,), F32),
+            pltpu.SMEM((16,), F32),
+            pltpu.SMEM((1,), F32),
             pltpu.VMEM((NA, 2 * HALF), BF16),
             pltpu.VMEM((NB, HALF), BF16),
             pltpu.VMEM((27, 3, 16), BF16),
@@ -383,11 +399,11 @@
             pltpu.VMEM((12 * WB, 768), BF16),
             pltpu.VMEM((BLOCKS, 3, 11 * WB, 256), BF16),
             pltpu.VMEM((10 * WB, 1536), BF16),
-            pltpu.SemaphoreType.DMA((5,)),
+            pltpu.SemaphoreType.DMA((10,)),
             pltpu.SemaphoreType.DMA((10,)),
         ],
         compiler_params=pltpu.CompilerParams(
-            collective_id=0, has_side_effects=True, vmem_limit_bytes=48 * 1024 * 1024
+            collective_id=0, has_side_effects=True, vmem_limit_bytes=60 * 1024 * 1024
         ),
         name="pair_scores",
     )(owner, valid, b_first, b_middle, b_last, bank, feats, wf, wm, wl)

time: 42.4 us -> 36.8 us (0.87)
  local copies, waits for them, and re-layouts: 5.7 us -> 0.63 us
    unnamed x15 -> x1, local copies, waits for them, and re-layouts: 5.7 us -> 0.63 us
where the time goes in v3:
time: 36.8 us; the launch traced here: 36.6 us
  Pallas kernels  34.1 us (93%)
  between operations  1.95 us (5%)
  local copies, waits for them, and re-layouts  0.63 us (2%)
    pallas_call x1, Pallas kernels, score(): pl.pallas_call(functools.partial(kernel, sizes), out_shape=pltpu.VMEM((1,...  34.1 us

profile of v3, /device:TPU:1, one launch (start us, length us, event | category | flops | bytes accessed | tf_op | source)
XLA Modules:
  0.0 36.6 jit_solution(12898799329289517927)
XLA Ops:
  1.9 34.1 %pair_scores.1 = f32[1,64,256]{2,1,0:T(8,128)S(1)} custom-call(s32[1]{0:T(128)S(6)} %copy.13.owner_hbm, s32[1]{0:T(128)S(6)} %copy.14.valid_hbm, f32[16]{0:T(128)} %bf_hbm.1, f32[16]{0:T(128)} %bm_hbm.1, f32[1]{0:T(128)S(6)} %copy.15.bl_hbm, bf16[1,64,1024]{2,1,0:T(8,128)(2,1)} %q_hbm.1, bf16[1,512,512]{2,1,0:T(8,128)(2,1)} %t_hbm.1, ...), custom_call_target="tpu_custom_call" | custom-call | tf_op jit(solution)/shard_map/pair_scores/pallas_call | solution.py:366
  36.0 0.6 %copy.12 = f32[1,64,256]{2,1,0:T(8,128)} copy(f32[1,64,256]{2,1,0:T(8,128)S(1)} %pair_scores.1) | data formatting | bytes 131072

commit v4 on v3

--- a/solution.py
+++ b/solution.py
@@ -22,6 +22,7 @@
 BLOCKS = 6
 STEP = 6
 HALF = 512
+CHUNKS = 2
 
 
 def nt(left, right):
@@ -175,20 +176,28 @@
     def at(g_of, z_of):
         return ((g_of // inner) * depth + z_of) * inner + lax.rem(g_of, inner)
 
-    def in_group(o):
-        return at(lax.rem(g + o, group), z)
-
-    def along(o):
-        return at(g, lax.rem(z + o, depth))
+    cores, columns = min(2, inner), max(1, inner // 2)
+    layers = group // inner
+    core, x, layer = lax.rem(g, cores), lax.rem(g // cores, columns), g // inner
+    steps = [(dy, dx, dc) for dy in range(layers) for dx in range(columns) for dc in range(cores)]
+    steps = sorted(steps, key=lambda s: (-s[0] - min(s[1], columns - s[1]), -s[2]))[:-1]
+    members = [
+        (lax.rem(layer + dy, layers) * columns + lax.rem(x + dx, columns)) * cores + lax.rem(core + dc, cores)
+        for dy, dx, dc in steps
+    ]
+    others = [
+        lax.rem(z + o, depth) for o in sorted(range(1, depth), key=lambda o: -min(o, depth - o))
+    ]
 
     barrier = pltpu.get_barrier_semaphore()
 
     def greet(pair, trow):
         pl.semaphore_signal(barrier, inc=1, device_id=(pair, trow), device_id_type=MESH)
 
-    pl.loop(1, depth)(lambda o: greet(along(o), plane))
-    if group > 1:
-        pl.loop(1, group)(lambda o: greet(in_group(o), plane))
+    for other in others:
+        greet(at(g, other), plane)
+    for member in members:
+        greet(at(member, z), plane)
     greet(me, 1 - plane)
 
     local = [
@@ -241,11 +250,9 @@
     owner_g = (owner // (inner * depth)) * inner + lax.rem(owner, inner)
     owner_z = lax.rem(owner // inner, depth)
 
-    if group > 1:
-        pl.loop(1, group)(
-            lambda o: send(unit.at[lax.rem(g + o, group)], recv_a.at[g], 0, in_group(o), plane) and None
-        )
-    squares = send(sq_own, sq_oth, 4, me, 1 - plane)
+    for member in members:
+        send(unit.at[member], recv_a.at[g], 0, at(member, z), plane)
+    squares = send(sq_own, sq_oth, 3, me, 1 - plane)
     recv_a[g] = unit[g]
     if group > 1:
         wait(recv_a.at[pl.ds(0, group - 1)], 1)
@@ -253,14 +260,16 @@
     cand[...] = chosen
     recv_b[z] = chosen
 
-    pl.loop(1, depth)(lambda o: send(cand, recv_b.at[z], 1, along(o), plane) and None)
+    for other in others:
+        send(cand, recv_b.at[z], 1, at(g, other), plane)
     wait(recv_b.at[pl.ds(0, depth - 1)], 3)
     chosen = recv_b[owner_z]
     piece[...] = chosen
     gath[g] = chosen
 
+    for member in members:
+        send(piece, gath.at[g], 2, at(member, z), plane)
     if group > 1:
-        pl.loop(1, group)(lambda o: send(piece, gath.at[g], 2, in_group(o), plane) and None)
         wait(gath.at[pl.ds(0, group - 1)], 5)
     lines = []
     for line in range(8):
@@ -272,10 +281,14 @@
     window = jnp.concatenate(lines, axis=0).astype(BF16)
 
     blank = jnp.zeros((NA, HALF), BF16)
-    part[...] = nt(t_ref[0:256, :], jnp.concatenate([window, blank], axis=0)) + nt(
-        t_ref[256:512, :], jnp.concatenate([blank, window], axis=0)
-    )
-    partial = send(part, part_oth, 3, me, 1 - plane)
+    partial = []
+    for c in range(CHUNKS):
+        first = c * (256 // CHUNKS)
+        last = first + 256 // CHUNKS
+        part[first:last] = nt(t_ref[first:last, :], jnp.concatenate([window, blank], axis=0)) + nt(
+            t_ref[256 + first : 256 + last, :], jnp.concatenate([blank, window], axis=0)
+        )
+        partial.append(send(part.at[pl.ds(first, 256 // CHUNKS)], part_oth.at[pl.ds(first, 256 // CHUNKS)], 4 + c, me, 1 - plane))
 
     b1 = bias_row(bf_ref, 256)
     b2 = bias_row(bm_ref, 32 * STEP)
@@ -287,7 +300,8 @@
     inverse = lax.rsqrt(jnp.concatenate(columns, axis=0) + EPS_NORM)
     live = iota((NB, 128), 0) // WB < valid_ref[0]
 
-    partial.wait()
+    for copy in partial:
+        copy.wait()
     both = part[...] + part_oth[...]
     swapped = pltpu.roll(both, 64, 1)
     low = iota((256, 128), 1) < 64
@@ -400,7 +414,7 @@
             pltpu.VMEM((BLOCKS, 3, 11 * WB, 256), BF16),
             pltpu.VMEM((10 * WB, 1536), BF16),
             pltpu.SemaphoreType.DMA((10,)),
-            pltpu.SemaphoreType.DMA((10,)),
+            pltpu.SemaphoreType.DMA((8 + 2 * CHUNKS,)),
         ],
         compiler_params=pltpu.CompilerParams(
             collective_id=0, has_side_effects=True, vmem_limit_bytes=60 * 1024 * 1024

time: 36.8 us -> 36.1 us (0.981)
  Pallas kernels: 34.1 us -> 33.4 us
    pallas_call x1, Pallas kernels: 34.1 us -> 33.4 us  [score(): pl.pallas_call(functools.partial(kernel, sizes), out_shape=pltpu.VMEM((1,...]
where the time goes in v4:
time: 36.1 us; the launch traced here: 36 us
  Pallas kernels  33.4 us (93%)
  between operations  1.95 us (5%)
  local copies, waits for them, and re-layouts  0.63 us (2%)
    pallas_call x1, Pallas kernels, score(): pl.pallas_call(functools.partial(kernel, sizes), out_shape=pltpu.VMEM((1,...  33.4 us

profile of v4, /device:TPU:1, one launch (start us, length us, event | category | flops | bytes accessed | tf_op | source)
XLA Modules:
  0.0 36.0 jit_solution(9806868163160904037)
XLA Ops:
  1.9 33.4 %pair_scores.1 = f32[1,64,256]{2,1,0:T(8,128)S(1)} custom-call(s32[1]{0:T(128)S(6)} %copy.13.owner_hbm, s32[1]{0:T(128)S(6)} %copy.14.valid_hbm, f32[16]{0:T(128)} %bf_hbm.1, f32[16]{0:T(128)} %bm_hbm.1, f32[1]{0:T(128)S(6)} %copy.15.bl_hbm, bf16[1,64,1024]{2,1,0:T(8,128)(2,1)} %q_hbm.1, bf16[1,512,512]{2,1,0:T(8,128)(2,1)} %t_hbm.1, ...), custom_call_target="tpu_custom_call" | custom-call | tf_op jit(solution)/shard_map/pair_scores/pallas_call | solution.py:380
  35.4 0.6 %copy.12 = f32[1,64,256]{2,1,0:T(8,128)} copy(f32[1,64,256]{2,1,0:T(8,128)S(1)} %pair_scores.1) | data formatting | bytes 131072

commit v5 on v4

--- a/solution.py
+++ b/solution.py
@@ -73,33 +73,22 @@
                 w1[k, 32 * l : 32 * l + 32, 128 * tile : 128 * tile + 128] = block.astype(BF16)
 
     spread[0:216, :] = spread_rows(wl_ref, tmp)
-    w3[...] = jnp.zeros_like(w3)
-    odd1 = (iota((1, 128), 1) // 16) % 2 == 1
-    for half in range(2):
-        for tile in range(12):
-            m, first = tile // 2, (tile % 2) * 4
-            columns = [6 * m + q for q in range(first, first + 4) if q < STEP and 6 * m + q < WA]
-            if not columns or columns[-1] < 16 * half - 1 or columns[0] > 16 * half + 16:
-                continue
-            q_of = first + iota((16, 128), 1) // 32
-            c_in = 6 * m + q_of
-            j_of = c_in - (16 * half + iota((16, 128), 0)) + 1
-            j_of = jnp.where((q_of < STEP) & (c_in < WA), j_of, -1)
-            for k in range(3):
-                for l in range(3):
-                    for ra in range(2):
-                        block = jnp.zeros((16, 128), F32)
-                        for j in range(3):
-                            t0 = ((1 - ra) * 3 + j) * 3 + k
-                            t1 = ((2 - ra) * 3 + j) * 3 + k
-                            value = jnp.where(
-                                odd1,
-                                spread[8 * t1 + l : 8 * t1 + l + 1, :],
-                                spread[8 * t0 + l : 8 * t0 + l + 1, :],
-                            )
-                            block = jnp.where(j_of == j, value, block)
-                        at = 64 * l + 32 * ra + 16 * half
-                        w3[k, at : at + 16, 128 * tile : 128 * tile + 128] = block.astype(BF16)
+    row = iota((16, 128), 0)
+    lane = iota((16, 128), 1)
+    i_of = (lane // 16) % 2 - row // 8 + 1
+    for tile in range(2):
+        q_of = tile * 4 + lane // 32
+        j_of = jnp.where(q_of < STEP, q_of - row % 8 + 2, -1)
+        for k in range(3):
+            for l in range(3):
+                block = jnp.zeros((16, 128), F32)
+                for i in range(3):
+                    for j in range(3):
+                        t = (i * 3 + j) * 3 + k
+                        value = spread[8 * t + l : 8 * t + l + 1, :]
+                        block = jnp.where((j_of == j) & (i_of == i), value, block)
+                at = 16 * (3 * k + l)
+                w3[at : at + 16, 128 * tile : 128 * tile + 128] = block.astype(BF16)
 
     take = (iota((16, 128), 1) % 16 == iota((16, 128), 0)).astype(F32).astype(BF16)
     spread[...] = nn(wm_ref[...].reshape(81 * 16, 16), take)
@@ -165,7 +154,7 @@
     sizes, owner_hbm, valid_hbm, bf_hbm, bm_hbm, bl_hbm, q_hbm, t_hbm, wf_hbm, wm_hbm, wl_hbm,
     out_ref,
     owner_ref, valid_ref, bf_ref, bm_ref, bl_ref, q_ref, t_ref, wf_ref, wm_ref, wl_ref, unit, recv_a, cand, recv_b, piece, gath, sq_own, sq_oth, part, part_oth,
-    tmp, spread, w1, w2, w3, e_ref, vbuf, xbuf, h1, h2, loads, sems,
+    tmp, spread, w1, w2, w3, e_ref, vbuf, xbuf, h1, h2, total, loads, sems,
 ):
     group, depth, inner, rows = sizes
     me = lax.axis_index("pair")
@@ -295,8 +284,8 @@
     squares.wait()
     columns = []
     for t in range(4):
-        total = sq_own[t : t + 1, :] + sq_oth[t : t + 1, :]
-        columns.append(jnp.transpose(jnp.broadcast_to(total, (128, 128))))
+        both = sq_own[t : t + 1, :] + sq_oth[t : t + 1, :]
+        columns.append(jnp.transpose(jnp.broadcast_to(both, (128, 128))))
     inverse = lax.rsqrt(jnp.concatenate(columns, axis=0) + EPS_NORM)
     live = iota((NB, 128), 0) // WB < valid_ref[0]
 
@@ -346,19 +335,29 @@
             for l in range(3):
                 acc = acc + nt(h1[m, l, WB * k : WB * k + 9 * WB, :], w2[3 * k + l])
         hidden = jnp.maximum(acc + b2, 0.0)
+        if m == BLOCKS - 1:
+            hidden = jnp.where(iota((9 * WB, 256), 1) < 32 * (WA - STEP * m), hidden, 0.0)
         h2[pl.ds(edge, WB), 256 * m : 256 * m + 256] = jnp.zeros((WB, 256), BF16)
         h2[pl.ds(pad, 9 * WB), 256 * m : 256 * m + 256] = hidden.astype(BF16)
 
-    acc = nt(w3[0], h2[0 : 8 * WB, :])
-    for k in (1, 2):
-        acc = acc + nt(w3[k], h2[WB * k : WB * k + 8 * WB, :])
-    column = iota((NA, 8 * WB), 1) % WB
-    result = acc[NA : 2 * NA]
-    result = result + jnp.where(column == 0, 0.0, pltpu.roll(acc[0:NA], 1, 1))
-    result = result + jnp.where(column == WB - 1, 0.0, pltpu.roll(acc[2 * NA : 3 * NA], 8 * WB - 1, 1))
-    result = result + bl_ref[0]
-    row = plane * 8 + iota((NA, 8 * WB), 1) // WB
-    out_ref[0] = jnp.where(row < valid_ref[0], result, 0.0)
+    column = iota((16, 8 * WB), 1) % WB
+    total[...] = jnp.zeros_like(total)
+    for m in range(BLOCKS):
+        acc = nt(w3[...], h2[:, 256 * m : 256 * m + 256])
+        sums = []
+        for l in range(3):
+            terms = [acc[16 * (3 * k + l) : 16 * (3 * k + l) + 16] for k in range(3)]
+            moved = [terms[0]] + [pltpu.roll(terms[k], 12 * WB - WB * k, 1) for k in (1, 2)]
+            sums.append(moved[0][:, 0 : 8 * WB] + moved[1][:, 0 : 8 * WB] + moved[2][:, 0 : 8 * WB])
+        block = sums[1]
+        block = block + jnp.where(column == 0, 0.0, pltpu.roll(sums[0], 1, 1))
+        block = block + jnp.where(column == WB - 1, 0.0, pltpu.roll(sums[2], 8 * WB - 1, 1))
+        for ra in range(2):
+            total[ra, STEP * m : STEP * m + 8, :] += block[8 * ra : 8 * ra + 8]
+    row = plane * 8 + iota((WA, 8 * WB), 1) // WB
+    for ra in range(2):
+        result = total[ra, 1 : 1 + WA, :] + bl_ref[0]
+        out_ref[0, WA * ra : WA * ra + WA, :] = jnp.where(row < valid_ref[0], result, 0.0)
 
     if group > 1:
         wait(recv_a.at[pl.ds(0, group - 1)], 0)
@@ -407,12 +406,13 @@
             pltpu.VMEM((81 * 16, 128), F32),
             pltpu.VMEM((3, 128, 256), BF16),
             pltpu.VMEM((9, 256, 256), BF16),
-            pltpu.VMEM((3, 192, 1536), BF16),
+            pltpu.VMEM((144, 256), BF16),
             pltpu.VMEM((256, 768), BF16),
             pltpu.VMEM((NB + 2 * WB, 256), BF16),
             pltpu.VMEM((12 * WB, 768), BF16),
             pltpu.VMEM((BLOCKS, 3, 11 * WB, 256), BF16),
-            pltpu.VMEM((10 * WB, 1536), BF16),
+            pltpu.VMEM((12 * WB, 1536), BF16),
+            pltpu.VMEM((2, 40, 8 * WB), F32),
             pltpu.SemaphoreType.DMA((10,)),
             pltpu.SemaphoreType.DMA((8 + 2 * CHUNKS,)),
         ],

time: 36.1 us -> 35 us (0.970)
  Pallas kernels: 33.4 us -> 32.3 us
    pallas_call x1, Pallas kernels: 33.4 us -> 32.3 us  [score(): pl.pallas_call(functools.partial(kernel, sizes), out_shape=pltpu.VMEM((1,...]
where the time goes in v5:
time: 35 us; the launch traced here: 34.9 us
  Pallas kernels  32.3 us (92%)
  between operations  1.95 us (6%)
  local copies, waits for them, and re-layouts  0.63 us (2%)
    pallas_call x1, Pallas kernels, score(): pl.pallas_call(functools.partial(kernel, sizes), out_shape=pltpu.VMEM((1,...  32.3 us

profile of v5, /device:TPU:1, one launch (start us, length us, event | category | flops | bytes accessed | tf_op | source)
XLA Modules:
  0.0 34.9 jit_solution(1983479511360656107)
XLA Ops:
  1.9 32.3 %pair_scores.1 = f32[1,64,256]{2,1,0:T(8,128)S(1)} custom-call(s32[1]{0:T(128)S(6)} %copy.13.owner_hbm, s32[1]{0:T(128)S(6)} %copy.14.valid_hbm, f32[16]{0:T(128)} %bf_hbm.1, f32[16]{0:T(128)} %bm_hbm.1, f32[1]{0:T(128)S(6)} %copy.15.bl_hbm, bf16[1,64,1024]{2,1,0:T(8,128)(2,1)} %q_hbm.1, bf16[1,512,512]{2,1,0:T(8,128)(2,1)} %t_hbm.1, ...), custom_call_target="tpu_custom_call" | custom-call | tf_op jit(solution)/shard_map/pair_scores/pallas_call | solution.py:379
  34.2 0.6 %copy.12 = f32[1,64,256]{2,1,0:T(8,128)} copy(f32[1,64,256]{2,1,0:T(8,128)S(1)} %pair_scores.1) | data formatting | bytes 131072

commit v6 on v5

--- a/solution.py
+++ b/solution.py
@@ -70,7 +70,8 @@
                             t = (i * 3 + j) * 3 + k
                             value = spread[8 * t + l : 8 * t + l + 1, :]
                             block = jnp.where((j_of == j) & (i_of == i), value, block)
-                w1[k, 32 * l : 32 * l + 32, 128 * tile : 128 * tile + 128] = block.astype(BF16)
+                at = 128 * k + 32 * l
+                w1[at : at + 32, 128 * tile : 128 * tile + 128] = block.astype(BF16)
 
     spread[0:216, :] = spread_rows(wl_ref, tmp)
     row = iota((16, 128), 0)
@@ -312,9 +313,8 @@
 
     lane = iota((10 * WB, 256), 1)
     for m in range(BLOCKS):
-        acc = nn(xbuf[0 : 10 * WB, 128 * m : 128 * m + 128], w1[0])
-        for k in (1, 2):
-            acc = acc + nn(xbuf[WB * k : WB * k + 10 * WB, 128 * m : 128 * m + 128], w1[k])
+        taps = [xbuf[WB * k : WB * k + 10 * WB, 128 * m : 128 * m + 128] for k in range(3)]
+        acc = nn(jnp.concatenate(taps[0:2], axis=1), w1[0:256, :]) + nn(taps[2], w1[256:384, :])
         hidden = jnp.maximum(acc + b1, 0.0)
         if m == 0:
             hidden = jnp.where(lane < 32, 0.0, hidden)
@@ -404,7 +404,7 @@
             pltpu.VMEM((256, 128), F32),
             pltpu.VMEM((27, 8, 128), F32),
             pltpu.VMEM((81 * 16, 128), F32),
-            pltpu.VMEM((3, 128, 256), BF16),
+            pltpu.VMEM((384, 256), BF16),
             pltpu.VMEM((9, 256, 256), BF16),
             pltpu.VMEM((144, 256), BF16),
             pltpu.VMEM((256, 768), BF16),

time: 35 us -> 34.8 us (level)
  no operation moved by 1% of the time
where the time goes in v6:
time: 34.8 us; the launch traced here: 34.6 us
  Pallas kernels  32.1 us (92%)
  between operations  1.95 us (6%)
  local copies, waits for them, and re-layouts  0.63 us (2%)
    pallas_call x1, Pallas kernels, score(): pl.pallas_call(functools.partial(kernel, sizes), out_shape=pltpu.VMEM((1,...  32.1 us

profile of v6, /device:TPU:1, one launch (start us, length us, event | category | flops | bytes accessed | tf_op | source)
XLA Modules:
  0.0 34.6 jit_solution(2817319846534649144)
XLA Ops:
  1.9 32.1 %pair_scores.1 = f32[1,64,256]{2,1,0:T(8,128)S(1)} custom-call(s32[1]{0:T(128)S(6)} %copy.13.owner_hbm, s32[1]{0:T(128)S(6)} %copy.14.valid_hbm, f32[16]{0:T(128)} %bf_hbm.1, f32[16]{0:T(128)} %bm_hbm.1, f32[1]{0:T(128)S(6)} %copy.15.bl_hbm, bf16[1,64,1024]{2,1,0:T(8,128)(2,1)} %q_hbm.1, bf16[1,512,512]{2,1,0:T(8,128)(2,1)} %t_hbm.1, ...), custom_call_target="tpu_custom_call" | custom-call | tf_op jit(solution)/shard_map/pair_scores/pallas_call | solution.py:379
  34.0 0.6 %copy.12 = f32[1,64,256]{2,1,0:T(8,128)} copy(f32[1,64,256]{2,1,0:T(8,128)S(1)} %pair_scores.1) | data formatting | bytes 131072

commit v7 on v6

--- a/solution.py
+++ b/solution.py
@@ -280,6 +280,8 @@
         )
         partial.append(send(part.at[pl.ds(first, 256 // CHUNKS)], part_oth.at[pl.ds(first, 256 // CHUNKS)], 4 + c, me, 1 - plane))
 
+    vbuf[0:WB, :] = jnp.zeros((WB, 128), F32)
+    vbuf[WB + NB : 2 * WB + NB, :] = jnp.zeros((WB, 128), F32)
     b1 = bias_row(bf_ref, 256)
     b2 = bias_row(bm_ref, 32 * STEP)
     squares.wait()
@@ -297,17 +299,15 @@
     low = iota((256, 128), 1) < 64
     raw = jnp.concatenate([jnp.where(low, both, swapped), jnp.where(low, swapped, both)], axis=0)
     corr = jnp.where(live, math.sqrt(1024) * raw * inverse, 0.0)
-    magnitude = jnp.abs(corr)
-    peak_query = jnp.max(magnitude, axis=1, keepdims=True)
-    peak_target = jnp.max(magnitude, axis=0, keepdims=True)
-    volume = corr * (corr * (1.0 / (peak_query + EPS_PEAK))) * (corr * (1.0 / (peak_target + EPS_PEAK)))
-    vbuf[0:WB, :] = jnp.zeros((WB, 256), BF16)
-    vbuf[WB + NB : 2 * WB + NB, :] = jnp.zeros((WB, 256), BF16)
-    low = iota((NB, 128), 1) < 64
-    vbuf[WB : WB + NB, 0:128] = jnp.where(low, shifted(volume, 1, 0), volume).astype(BF16)
-    vbuf[WB : WB + NB, 128:256] = shifted(volume, -1, WB - 1).astype(BF16)
+    peak_target = jnp.max(jnp.abs(corr), axis=0, keepdims=True)
+    vbuf[WB : WB + NB, :] = corr
     start = pl.multiple_of(plane * (6 * WB), 6 * WB)
-    xbuf[...] = nn(vbuf[pl.ds(start, 12 * WB), :], e_ref[...]).astype(BF16)
+    near = vbuf[pl.ds(start, 12 * WB), :]
+    peak_query = jnp.max(jnp.abs(near), axis=1, keepdims=True)
+    volume = near * (near * (1.0 / (peak_query + EPS_PEAK))) * (near * (1.0 / (peak_target + EPS_PEAK)))
+    low = iota((12 * WB, 128), 1) < 64
+    chosen = [jnp.where(low, shifted(volume, 1, 0), volume), shifted(volume, -1, WB - 1)]
+    xbuf[...] = nn(jnp.concatenate(chosen, axis=1).astype(BF16), e_ref[...]).astype(BF16)
 
     pad = pl.multiple_of((1 - plane) * WB, WB)
 
@@ -408,7 +408,7 @@
             pltpu.VMEM((9, 256, 256), BF16),
             pltpu.VMEM((144, 256), BF16),
             pltpu.VMEM((256, 768), BF16),
-            pltpu.VMEM((NB + 2 * WB, 256), BF16),
+            pltpu.VMEM((NB + 2 * WB, 128), F32),
             pltpu.VMEM((12 * WB, 768), BF16),
             pltpu.VMEM((BLOCKS, 3, 11 * WB, 256), BF16),
             pltpu.VMEM((12 * WB, 1536), BF16),

time: 34.8 us -> 34.9 us (level)
  no operation moved by 1% of the time
where the time goes in v7:
time: 34.9 us; the launch traced here: 34.7 us
  Pallas kernels  32.2 us (92%)
  between operations  1.95 us (6%)
  local copies, waits for them, and re-layouts  0.63 us (2%)
    pallas_call x1, Pallas kernels, score(): pl.pallas_call(functools.partial(kernel, sizes), out_shape=pltpu.VMEM((1,...  32.2 us

profile of v7, /device:TPU:1, one launch (start us, length us, event | category | flops | bytes accessed | tf_op | source)
XLA Modules:
  0.0 34.7 jit_solution(16799901543381302379)
XLA Ops:
  1.9 32.2 %pair_scores.1 = f32[1,64,256]{2,1,0:T(8,128)S(1)} custom-call(s32[1]{0:T(128)S(6)} %copy.13.owner_hbm, s32[1]{0:T(128)S(6)} %copy.14.valid_hbm, f32[16]{0:T(128)} %bf_hbm.1, f32[16]{0:T(128)} %bm_hbm.1, f32[1]{0:T(128)S(6)} %copy.15.bl_hbm, bf16[1,64,1024]{2,1,0:T(8,128)(2,1)} %q_hbm.1, bf16[1,512,512]{2,1,0:T(8,128)(2,1)} %t_hbm.1, ...), custom_call_target="tpu_custom_call" | custom-call | tf_op jit(solution)/shard_map/pair_scores/pallas_call | solution.py:379
  34.1 0.6 %copy.12 = f32[1,64,256]{2,1,0:T(8,128)} copy(f32[1,64,256]{2,1,0:T(8,128)S(1)} %pair_scores.1) | data formatting | bytes 131072
